TPU v7x, 32 devices: a whole 2x2x4 slice. The times are simulated.
32 devices in a mesh: vel: 16 (over z, y, x), space: 2 (over core).
Axes of the slice: x: 2, y: 2, z: 4, core: 2. Of those that a mesh axis runs over, the one named last changes fastest.
Arguments:
- distribution: float32 [16384, 16, 128], P('vel', 'space'), may hold values from 0 to 11, as said below
- rate_class: int32 [16, 128], P('space'), may hold values from 0 to 7
- boundary_obstacle_indicator: int32 [16, 128], P('space'), may hold values 0 or 1
Outputs:
- field_out: float32 [16384, 16, 128], P('vel', 'space')
- latest_conserved_fields: float32 [5, 16, 128], P(None, 'space')
Inputs may be any that keep to these rules, and one draw needn't show every extreme that they name: `distribution`: every entry positive.
All inputs are finite; a program needn't handle non-finite values. No bound on the sum of `boundary_obstacle_indicator` on one device may be relied on, other than what follows from the above.
Results may differ from a plain program's by a relative error of at most 0.0003.
Values sent between devices are 32-bit elements; how exact they have to be, the bound alone decides.
A program may use at most 64 MiB of HBM per device.

v0:
```python
import jax
import jax.numpy as jnp
from jax import lax
from jax.sharding import PartitionSpec as P

VX = 32
VY = 32
VZ = 16
ITERS = 2
SWEEPS = 4


speed_edge = 5.0
marching_step_length = 0.1
momentum_thermal_ratio = 2.0 / 3.0
shear_power_law_index = 0.81
diffusivity = 1.0


def with_halo(value, sides, width):
    for axis, dim in sides:
        size, length = (lax.axis_size(axis), value.shape[dim])
        up = [(i, (i + 1) % size) for i in range(size)]
        down = [(j, i) for i, j in up]
        last = lax.slice_in_dim(value, length - width, length, axis=dim)
        leading = lax.slice_in_dim(value, 0, width, axis=dim)
        before = lax.ppermute(last, axis, up)
        after = lax.ppermute(leading, axis, down)
        value = jnp.concatenate([before, value, after], axis=dim)
    return value


def velocity_table(index):
    index_x = index % VX
    index_y = index // VX % VY
    index_z = index // (VX * VY)
    discrete_abscissa_xaxis = -speed_edge + (index_x.astype(jnp.float32) + 0.5) * (
        2.0 * speed_edge / VX
    )
    discrete_abscissa_yaxis = -speed_edge + (index_y.astype(jnp.float32) + 0.5) * (
        2.0 * speed_edge / VY
    )
    discrete_abscissa_zaxis = -speed_edge + (index_z.astype(jnp.float32) + 0.5) * (
        2.0 * speed_edge / VZ
    )
    return (discrete_abscissa_xaxis, discrete_abscissa_yaxis, discrete_abscissa_zaxis)


def moment_weights(discrete_abscissa_xaxis, discrete_abscissa_yaxis, discrete_abscissa_zaxis):
    square = (
        discrete_abscissa_xaxis * discrete_abscissa_xaxis
        + discrete_abscissa_yaxis * discrete_abscissa_yaxis
        + discrete_abscissa_zaxis * discrete_abscissa_zaxis
    )
    quadrature = (
        2.0
        * speed_edge
        / VX
        * (2.0 * speed_edge / VY)
        * (2.0 * speed_edge / VZ)
        / (2.0 * jnp.pi) ** 1.5
    )
    rows = [
        jnp.ones_like(discrete_abscissa_xaxis),
        discrete_abscissa_xaxis,
        discrete_abscissa_yaxis,
        discrete_abscissa_zaxis,
        square,
        discrete_abscissa_xaxis * discrete_abscissa_xaxis,
        discrete_abscissa_yaxis * discrete_abscissa_yaxis,
        discrete_abscissa_xaxis * discrete_abscissa_yaxis,
        discrete_abscissa_xaxis * discrete_abscissa_zaxis,
        discrete_abscissa_yaxis * discrete_abscissa_zaxis,
        discrete_abscissa_xaxis * square,
        discrete_abscissa_yaxis * square,
        discrete_abscissa_zaxis * square,
    ]
    return jnp.stack(rows) * quadrature


def conserved(moments):
    return jnp.stack([moments[0], moments[1], moments[2], moments[3], 0.5 * moments[4]])


def heat_flux(moments):
    mass = moments[0]
    flow_x = moments[1] / mass
    flow_y = moments[2] / mass
    flow_z = moments[3] / mass
    p_xx = moments[5]
    p_yy = moments[6]
    p_zz = moments[4] - moments[5] - moments[6]
    p_xy = moments[7]
    p_xz = moments[8]
    p_yz = moments[9]
    flow_sq = flow_x * flow_x + flow_y * flow_y + flow_z * flow_z
    heat_x = 0.5 * (
        moments[10]
        - 2.0 * (flow_x * p_xx + flow_y * p_xy + flow_z * p_xz)
        - flow_x * moments[4]
        + 2.0 * mass * flow_sq * flow_x
    )
    heat_y = 0.5 * (
        moments[11]
        - 2.0 * (flow_x * p_xy + flow_y * p_yy + flow_z * p_yz)
        - flow_y * moments[4]
        + 2.0 * mass * flow_sq * flow_y
    )
    heat_z = 0.5 * (
        moments[12]
        - 2.0 * (flow_x * p_xz + flow_y * p_yz + flow_z * p_zz)
        - flow_z * moments[4]
        + 2.0 * mass * flow_sq * flow_z
    )
    return jnp.stack([heat_x, heat_y, heat_z])


def transport(field, courant_x, courant_y):
    from_left = jnp.roll(field, 1, 2)
    from_right = jnp.roll(field, -1, 2)
    term_y = jnp.where(
        courant_y > 0, courant_y * (field - from_left), courant_y * (from_right - field)
    )
    padded = with_halo(field, (("space", 1),), 1)
    term_x = jnp.where(
        courant_x > 0, courant_x * (field - padded[:, :-2]), courant_x * (padded[:, 2:] - field)
    )
    return field - term_x - term_y


def diffuse(source):
    margin = with_halo(source, (("space", 1),), SWEEPS)
    iterate = margin
    for sweep_index in range(SWEEPS):
        inner = iterate[:, 1:-1]
        beside = iterate[:, :-2] + iterate[:, 2:] + jnp.roll(inner, 1, 2) + jnp.roll(inner, -1, 2)
        margin_edge = sweep_index + 1
        iterate = (
            margin[:, margin_edge : margin.shape[1] - margin_edge] + diffusivity * beside
        ) / (1.0 + 4.0 * diffusivity)
    return iterate


def collision_update_piece(
    convected_fields,
    discrete_abscissa_xaxis,
    discrete_abscissa_yaxis,
    discrete_abscissa_zaxis,
    particle_concentration,
    mean_drift_velocity,
    kinetic_thermal_level,
    energy_flux_components,
    collision_frequency,
    obstacle_indicators,
):
    diff_x = discrete_abscissa_xaxis - mean_drift_velocity[0]
    diff_y = discrete_abscissa_yaxis - mean_drift_velocity[1]
    diff_z = discrete_abscissa_zaxis - mean_drift_velocity[2]
    quadratic_deviation = diff_x * diff_x + diff_y * diff_y + diff_z * diff_z
    prefactor_amplitude = particle_concentration * kinetic_thermal_level ** (-1.5)
    local_gaussian_population = prefactor_amplitude * jnp.exp(
        -0.5 * quadratic_deviation / kinetic_thermal_level
    )
    skewed_correction_multiplier = (1.0 - momentum_thermal_ratio) / (
        5.0 * particle_concentration * kinetic_thermal_level * kinetic_thermal_level
    )
    projected_energy_flux = (
        diff_x * energy_flux_components[0]
        + diff_y * energy_flux_components[1]
        + diff_z * energy_flux_components[2]
    )
    goal_population = local_gaussian_population * (
        1.0
        + skewed_correction_multiplier
        * projected_energy_flux
        * (quadratic_deviation / kinetic_thermal_level - 5.0)
    )
    wall_state = particle_concentration * jnp.exp(
        -0.5
        * (
            discrete_abscissa_xaxis * discrete_abscissa_xaxis
            + discrete_abscissa_yaxis * discrete_abscissa_yaxis
            + discrete_abscissa_zaxis * discrete_abscissa_zaxis
        )
    )
    relaxed = convected_fields + collision_frequency * (goal_population - convected_fields)
    return jnp.where(obstacle_indicators > 0, wall_state, relaxed)


def per_device(distribution, rate_class, boundary_obstacle_indicator):
    vel_count, row_count, col_count = distribution.shape
    index = lax.axis_index("vel") * vel_count + jnp.arange(vel_count, dtype=jnp.int32)
    discrete_abscissa_xaxis, discrete_abscissa_yaxis, discrete_abscissa_zaxis = velocity_table(
        index
    )
    weights = moment_weights(
        discrete_abscissa_xaxis, discrete_abscissa_yaxis, discrete_abscissa_zaxis
    )
    column_x = discrete_abscissa_xaxis[:, None, None]
    column_y = discrete_abscissa_yaxis[:, None, None]
    column_z = discrete_abscissa_zaxis[:, None, None]
    courant_x = marching_step_length * column_x
    courant_y = marching_step_length * column_y
    reference_collision_freq = 0.5 * jnp.exp2(rate_class.astype(jnp.float32))
    field = distribution
    latest_conserved_fields = jnp.zeros((5, row_count, col_count), jnp.float32)
    for step_index in range(ITERS):
        convected_fields = transport(field, courant_x, courant_y)
        partial_value = jnp.dot(
            weights,
            convected_fields.reshape(vel_count, row_count * col_count),
            precision=lax.Precision.HIGHEST,
            preferred_element_type=jnp.float32,
        )
        moments = lax.psum(partial_value, "vel")
        source = conserved(moments)
        energy_flux_components = heat_flux(moments)
        source = source.reshape(5, row_count, col_count)
        energy_flux_components = energy_flux_components.reshape(3, row_count, col_count)
        latest_conserved_fields = diffuse(source)
        particle_concentration = latest_conserved_fields[0]
        mean_drift_velocity = latest_conserved_fields[1:4] / particle_concentration
        kinetic_thermal_level = (
            2.0 * latest_conserved_fields[4] / particle_concentration
            - (
                mean_drift_velocity[0] * mean_drift_velocity[0]
                + mean_drift_velocity[1] * mean_drift_velocity[1]
                + mean_drift_velocity[2] * mean_drift_velocity[2]
            )
        ) / 3.0
        collision_frequency = 1.0 - jnp.exp(
            -marching_step_length
            * reference_collision_freq
            * particle_concentration
            * kinetic_thermal_level ** (1.0 - shear_power_law_index)
        )
        field = collision_update_piece(
            convected_fields,
            column_x,
            column_y,
            column_z,
            particle_concentration,
            mean_drift_velocity,
            kinetic_thermal_level,
            energy_flux_components,
            collision_frequency,
            boundary_obstacle_indicator,
        )
    return (field, latest_conserved_fields)


def solution(mesh):
    placed = (P("vel", "space", None), P("space", None), P("space", None))
    return jax.shard_map(
        per_device,
        mesh=mesh,
        in_specs=placed,
        out_specs=(P("vel", "space", None), P(None, "space", None)),
        check_vma=False,
    )
```

profile of v0, /device:TPU:0, one launch (start us, length us, event | category | flops | bytes accessed | tf_op | source)
XLA Modules:
  0.0 239.6 jit_solution(17886712523408883976)
XLA Ops:
  0.6 4.2 %fusion.177 = (f32[1024,1,128]{2,1,0:T(1,128)S(1)}, f32[1024,1,128]{2,1,0:T(1,128)S(1)}) fusion(f32[1024,8,128]{2,1,0:T(8,128)} %param.3), kind=kLoop, calls=%fused_computation.291 | loop fusion | bytes 2097152 | tf_op jit(solution)/shard_map/slice | solution.py:25
  4.8 0.6 collective-permute-start.1
  6.1 5.4 %copy.27 = f32[1024,8,128]{0,2,1:T(8,128)} copy(f32[1024,8,128]{2,1,0:T(8,128)} %param.3) | data formatting | bytes 8388608 | tf_op args[0]
  11.4 1.1 fusion.176
  12.6 8.7 %fusion.175 = (f32[1024,8,127]{0,2,1:T(8,128)}, f32[1024,8,127]{0,2,1:T(8,128)}) fusion(f32[1024,8,128]{0,2,1:T(8,128)} %copy.27), kind=kLoop, calls=%fused_computation.289 | loop fusion | bytes 16646144 | tf_op jit(solution)/shard_map/jit(_roll_static)/slice | solution.py:120
  21.4 0.2 copy.25
  21.6 0.2 copy.20
  21.8 8.6 %fusion.47 = f32[1024,8,128]{0,2,1:T(8,128)S(1)} fusion(f32[1024,8,128]{0,2,1:T(8,128)} %copy.27, f32[1024,1,128]{0,2,1:T(8,128)S(1)} %copy.25, f32[1024,1,128]{0,2,1:T(8,128)S(1)} %copy.20, f32[1024,8,127]{0,2,1:T(8,128)} %get-tuple-element.17, f32[1024,8,1]{0,2,1:T(1,128)S(1)} %get-tuple-element.19, f32[1024,8,1]{0,2,1:T(1,128)S(1)} %get-tuple-element.18, ...), kind=kLoop, calls=%fused_computation.62 | loop fusion | flops 16777216 | bytes 17836032 | tf_op jit(solution)/shard_map/sub | solution.py:128
  30.4 2.0 copy-done.2
  32.4 3.6 %fusion.58 = f32[13,1024]{1,0:T(8,128)S(1)} fusion(f32[1024,1024]{0,1:T(8,128)S(1)} %bitcast.95, f32[13,1024]{1,0:T(8,128)S(1)} %stack.16), kind=kOutput, calls=%fused_computation.78 | convolution fusion | flops 163591168 | bytes 4300800 | tf_op jit(solution)/shard_map/dot_general | solution.py:209
  36.0 78.6 %psum.14 = f32[13,1024]{1,0:T(8,128)S(1)} all-reduce(f32[13,1024]{1,0:T(8,128)S(1)} %fusion.58), channel_id=1, replica_groups=mesh['vel'=16,'space'=2] {'vel'}, use_global_device_ids=true, to_apply=%region_0.1 | all-reduce | flops 13312 | bytes 106496 | tf_op jit(solution)/shard_map/psum | solution.py:215
  114.8 0.5 collective-permute-start.3
  115.3 0.6 collective-permute-done.2
  115.9 0.2 collective-permute-done.3
  117.2 7.4 %fusion.11 = f32[1024,8,128]{0,2,1:T(8,128)S(1)} fusion(f32[1024,8,128]{0,2,1:T(8,128)} %copy-done.2, f32[8,128]{1,0:T(8,128)S(1)} %bitcast.117, f32[8,128]{1,0:T(8,128)S(1)} %bitcast.115, f32[8,128]{1,0:T(8,128)S(1)} %bitcast.114, f32[8,128]{1,0:T(8,128)S(1)} %fusion.113, f32[8,128]{1,0:T(8,128)S(1)} %bitcast.111, f32[8,128]{1,0:T(8,128)S(1)} %get-tuple-element.71, ...), kind=kLoop, calls=%fused_computation.23 | loop fusion | flops 28311552 | bytes 8451072 | tf_op jit(solution)/shard_map/jit(_where)/select_n | solution.py:187
  124.7 1.9 copy-done
  126.7 0.2 copy.34
  126.9 0.2 copy.36
  127.1 0.4 collective-permute-start.5
  127.5 0.2 collective-permute-start.4
  127.7 8.7 %fusion.172 = (f32[1024,8,127]{0,2,1:T(8,128)}, f32[1024,8,127]{0,2,1:T(8,128)}) fusion(f32[1024,8,128]{0,2,1:T(8,128)} %copy-done), kind=kLoop, calls=%fused_computation.286 | loop fusion | bytes 16646144 | tf_op jit(solution)/shard_map/jit(_roll_static)/slice | solution.py:120
  136.5 0.2 copy.37
  136.7 0.2 copy.35
  136.9 8.6 %fusion.40 = f32[1024,8,128]{0,2,1:T(8,128)S(1)} fusion(f32[1024,8,128]{0,2,1:T(8,128)} %copy-done, f32[1024,1,128]{0,2,1:T(8,128)S(1)} %copy.37, f32[1024,1,128]{0,2,1:T(8,128)S(1)} %copy.35, f32[1024,8,127]{0,2,1:T(8,128)} %get-tuple-element.11, f32[1024,8,1]{0,2,1:T(1,128)S(1)} %get-tuple-element.13, f32[1024,8,1]{0,2,1:T(1,128)S(1)} %get-tuple-element.12, ...), kind=kLoop, calls=%fused_computation.53 | loop fusion | flops 16777216 | bytes 17836032 | tf_op jit(solution)/shard_map/sub | solution.py:128
  145.5 2.0 copy-done.1
  147.5 3.6 %fusion.56 = f32[13,1024]{1,0:T(8,128)S(1)} fusion(f32[1024,1024]{0,1:T(8,128)S(1)} %bitcast.94, f32[13,1024]{1,0:T(8,128)S(1)} %stack.16), kind=kOutput, calls=%fused_computation.76 | convolution fusion | flops 163591168 | bytes 4300800 | tf_op jit(solution)/shard_map/dot_general | solution.py:209
  151.1 71.8 %psum.15 = f32[13,1024]{1,0:T(8,128)S(1)} all-reduce(f32[13,1024]{1,0:T(8,128)S(1)} %fusion.56), channel_id=1, replica_groups=mesh['vel'=16,'space'=2] {'vel'}, use_global_device_ids=true, to_apply=%region_1.2 | all-reduce | flops 13312 | bytes 106496 | tf_op jit(solution)/shard_map/psum | solution.py:215
  223.0 0.5 collective-permute-start.7
  223.6 0.6 collective-permute-done.6
  224.2 0.2 collective-permute-done.7
  225.5 8.8 %fusion.29 = f32[1024,8,128]{0,2,1:T(8,128)} fusion(f32[1024,8,128]{0,2,1:T(8,128)} %copy-done.1, f32[8,128]{1,0:T(8,128)S(1)} %bitcast.116, f32[8,128]{1,0:T(8,128)S(1)} %bitcast.113, f32[8,128]{1,0:T(8,128)S(1)} %bitcast.112, f32[8,128]{1,0:T(8,128)S(1)} %fusion.115, f32[8,128]{1,0:T(8,128)S(1)} %bitcast.110, f32[8,128]{1,0:T(8,128)S(1)} %get-tuple-element.68, ...), kind=kLoop, calls=%fused_computation.41 | loop fusion | flops 28311552 | bytes 8451072 | tf_op jit(solution)/shard_map/jit(_where)/select_n | solution.py:187
  234.3 5.4 %copy.38 = f32[1024,8,128]{2,1,0:T(8,128)} copy(f32[1024,8,128]{0,2,1:T(8,128)} %fusion.29) | data formatting | bytes 8388608
  (77 shorter events, 3.5 us)
Async XLA Ops:
  4.8 16.6 %collective-permute-start.1 = (f32[1024,1,128]{2,0,1:T(8,128)S(1)}, f32[1024,1,128]{2,0,1:T(8,128)S(1)}, u32[]{:S(2)}, u32[]{:S(2)}) collective-permute-start(f32[1024,1,128]{2,0,1:T(8,128)S(1)} %bitcast.97), channel_id=1, source_target_pairs={{1,0},{0,1},{3,2},{2,3},{5,4},{4,5},{7,6},{6,7},{9,8},{8,9},{11,10... | collective-permute-start | bytes 1572872 | tf_op jit(solution)/shard_map/ppermute | solution.py:28
  5.4 16.2 %collective-permute-start = (f32[1024,1,128]{2,0,1:T(8,128)S(1)}, f32[1024,1,128]{2,0,1:T(8,128)S(1)}, u32[]{:S(2)}, u32[]{:S(2)}) collective-permute-start(f32[1024,1,128]{2,0,1:T(8,128)S(1)} %bitcast.96), channel_id=1, source_target_pairs={{0,1},{1,0},{2,3},{3,2},{4,5},{5,4},{6,7},{7,6},{8,9},{9,8},{10,11... | collective-permute-start | bytes 1572872 | tf_op jit(solution)/shard_map/ppermute | solution.py:27
  6.1 5.4 %copy-start.5 = (s32[8,128]{1,0:T(8,128)S(1)}, s32[8,128]{1,0:T(8,128)}, u32[]{:S(2)}) copy-start(s32[8,128]{1,0:T(8,128)} %param.5) | copy-start | bytes 12292
  30.4 2.0 copy-start.2
  30.4 86.7 %copy-start.4 = (s32[8,128]{1,0:T(8,128)S(1)}, s32[8,128]{1,0:T(8,128)}, u32[]{:S(2)}) copy-start(s32[8,128]{1,0:T(8,128)} %param.4) | copy-start | bytes 12292
  114.7 1.2 collective-permute-start.2
  114.8 1.3 collective-permute-start.3
  124.6 2.0 copy-start
  127.1 9.3 %collective-permute-start.5 = (f32[1024,1,128]{2,0,1:T(8,128)S(1)}, f32[1024,1,128]{2,0,1:T(8,128)S(1)}, u32[]{:S(2)}, u32[]{:S(2)}) collective-permute-start(f32[1024,1,128]{2,0,1:T(8,128)S(1)} %copy.36), channel_id=1, source_target_pairs={{1,0},{0,1},{3,2},{2,3},{5,4},{4,5},{7,6},{6,7},{9,8},{8,9},{11,10... | collective-permute-start | bytes 1572872 | tf_op jit(solution)/shard_map/ppermute | solution.py:28
  127.5 9.1 %collective-permute-start.4 = (f32[1024,1,128]{2,0,1:T(8,128)S(1)}, f32[1024,1,128]{2,0,1:T(8,128)S(1)}, u32[]{:S(2)}, u32[]{:S(2)}) collective-permute-start(f32[1024,1,128]{2,0,1:T(8,128)S(1)} %copy.34), channel_id=1, source_target_pairs={{0,1},{1,0},{2,3},{3,2},{4,5},{5,4},{6,7},{7,6},{8,9},{9,8},{10,11... | collective-permute-start | bytes 1572872 | tf_op jit(solution)/shard_map/ppermute | solution.py:27
  145.5 2.0 copy-start.1
  222.9 1.2 collective-permute-start.6
  223.0 1.3 collective-permute-start.7
  225.4 8.9 %copy-start.3 = (f32[5,8,128]{2,1,0:T(8,128)}, f32[5,8,128]{2,1,0:T(8,128)S(1)}, u32[]{:S(2)}) copy-start(f32[5,8,128]{2,1,0:T(8,128)S(1)} %fusion.87) | copy-start | bytes 61444
where the time goes:
time: 240 us
  blocking collectives  150 us (62%)
  local copies, waits for them, and re-layouts  42.1 us (18%)
  other arithmetic  35.1 us (15%)
  matrix products  7.12 us (3%)
    psum x2, blocking collectives, per_device(): moments = lax.psum(partial_value, 'vel')  150 us
    slice x4, local copies, waits for them, and re-layouts, transport(): from_right = jnp.roll(field, -1, 2)  18.6 us
    sub x2, other arithmetic, transport(): return field - term_x - term_y  17.2 us
    unnamed x18, local copies, waits for them, and re-layouts  16.7 us
    select_n x2, other arithmetic, collision_update_piece(): return jnp.where(obstacle_indicators > 0, wall_state, relaxed)  16.2 us
    dot_general x2, matrix products, per_device(): jnp.dot(weights, convected_fields.reshape(vel_count, row_count * col_coun...  7.12 us
  transfers between devices with their start and end apart: 8, of which 4 were waited for; matrix products, arithmetic and copies ran while one was open for 10% of the time, Pallas kernels for 0%

commit v1 on v0

v1 whole, which is shorter than its diff:
```python
import functools

import jax
import jax.numpy as jnp
from jax import lax
from jax.experimental import pallas as pl
from jax.experimental.pallas import tpu as pltpu
from jax.sharding import PartitionSpec as P

VX = 32
VY = 32
VZ = 16
HX = VX // 2
ITERS = 2
SWEEPS = 4
EDGE = 5.0
STEP = 0.1
PRANDTL = 2.0 / 3.0
SHEAR = 0.81
DIFFUSIVITY = 1.0
QUAD = (
    (2.0 * EDGE / VX) * (2.0 * EDGE / VY) * (2.0 * EDGE / VZ) / (2.0 * 3.141592653589793) ** 1.5
)
MESH = pl.DeviceIdType.MESH
f32 = jnp.float32


def speed_x(ix):
    return -EDGE + (ix + 0.5) * (2.0 * EDGE / VX)


def speed_y(iy):
    return -EDGE + (iy.astype(f32) + 0.5) * (2.0 * EDGE / VY)


def speed_z(iz):
    return -EDGE + (iz.astype(f32) + 0.5) * (2.0 * EDGE / VZ)


def velocity_base(vel_index, vel_count):
    first = vel_index * vel_count
    return lax.rem(lax.div(first, VX), VY), lax.div(first, VX * VY)


def diffuse_rows(rows_ref, tr_ref, row_count):
    total = row_count + 2 * SWEEPS
    src = [rows_ref[i] for i in range(total)]
    cols = src[0].shape[1]
    state = list(src)
    for sweep in range(SWEEPS):
        new = list(state)
        for i in range(sweep + 1, total - sweep - 1):
            beside = (
                state[i - 1]
                + state[i + 1]
                + pltpu.roll(state[i], 1, 1)
                + pltpu.roll(state[i], cols - 1, 1)
            )
            new[i] = (src[i] + DIFFUSIVITY * beside) * (1.0 / (1.0 + 4.0 * DIFFUSIVITY))
        state = new
    sub = lax.broadcasted_iota(jnp.int32, src[0].shape, 0)
    for r in range(row_count):
        tr_ref[r] = jnp.where(sub < 5, state[SWEEPS + r], src[SWEEPS + r])


def macro_tables(tr_ref, rate_ref, wall_ref, tab_x, tab_y, iy0, iz, iy_count):
    q = [tr_ref[:, k, :] for k in range(8)]
    density = q[0]
    inv_density = 1.0 / density
    ux, uy, uz = q[1] * inv_density, q[2] * inv_density, q[3] * inv_density
    temperature = (2.0 * q[4] * inv_density - (ux * ux + uy * uy + uz * uz)) / 3.0
    frequency = 0.5 * jnp.exp2(rate_ref[...].astype(f32))
    power = jnp.exp((1.0 - SHEAR) * jnp.log(temperature))
    rate = 1.0 - jnp.exp(-STEP * frequency * density * power)
    wall = wall_ref[...] > 0
    inv_t = 1.0 / temperature
    root = lax.rsqrt(temperature)
    prefactor = density * (root * root * root)
    coef = (1.0 - PRANDTL) / (5.0 * density * temperature * temperature)
    hx, hy, hz = coef * q[5], coef * q[6], coef * q[7]
    zero = jnp.zeros_like(density)
    sz = jnp.full(density.shape, speed_z(iz), f32)
    cz = sz - uz
    z2 = cz * cz * inv_t
    scale_z = rate * prefactor * jnp.exp(-0.5 * z2)
    wall_z = density * jnp.exp(-0.5 * sz * sz)
    qz = hz * cz

    def table_x(ix, carry):
        sx = jnp.full(density.shape, speed_x(ix.astype(f32)), f32)
        cx = sx - ux
        x2 = cx * cx * inv_t
        tab_x[0, ix] = jnp.exp(-0.5 * jnp.where(wall, sx * sx, x2))
        tab_x[1, ix] = jnp.where(wall, zero, hx * cx)
        tab_x[2, ix] = jnp.where(wall, zero, x2)
        return carry

    lax.fori_loop(0, VX, table_x, 0, unroll=4)

    def table_y(iy, carry):
        sy = jnp.full(density.shape, speed_y(iy0 + iy), f32)
        cy = sy - uy
        y2 = cy * cy * inv_t
        tab_y[0, iy] = jnp.where(wall, wall_z, scale_z) * jnp.exp(
            -0.5 * jnp.where(wall, sy * sy, y2)
        )
        tab_y[1, iy] = jnp.where(wall, zero, hy * cy + qz)
        tab_y[2, iy] = jnp.where(wall, zero, y2 + z2 - 5.0)
        return carry

    lax.fori_loop(0, iy_count, table_y, 0, unroll=min(4, iy_count))
    return jnp.where(wall, zero, 1.0 - rate)


def collide(load, store, tab_x, tab_y, keep, start, count):
    block = 4 if count % 4 == 0 else 2 if count % 2 == 0 else 1

    def body(step, carry):
        base = start + step * block
        g = [tab_y[0, base + b] for b in range(block)]
        h = [tab_y[1, base + b] for b in range(block)]
        r = [tab_y[2, base + b] for b in range(block)]
        for ix in range(VX):
            ex, ax, bx = tab_x[0, ix], tab_x[1, ix], tab_x[2, ix]
            for b in range(block):
                old = load(base + b, ix)
                shape = (ax + h[b]) * (bx + r[b]) + 1.0
                store(base + b, ix, keep * old + (ex * g[b]) * shape)
        return carry

    lax.fori_loop(0, count // block, body, 0)


def chunks_of(iy_count):
    return 4 if iy_count % 4 == 0 else 1


def heat_row(total, z1, z2, z3):
    def at(array, k):
        return array[k : k + 1, :]

    m0, m1, m2, m3 = at(total, 0), at(total, 1), at(total, 2), at(z1, 0)
    m5, m6, m7 = at(total, 3), at(total, 4), at(total, 5)
    m4 = m5 + m6 + at(z2, 0)
    m8, m9 = at(z1, 1), at(z1, 2)
    m10 = at(total, 6) + at(z2, 1)
    m11 = at(total, 7) + at(z2, 2)
    m12 = at(z1, 3) + at(z1, 4) + at(z3, 0)
    inv = 1.0 / m0
    ux, uy, uz = m1 * inv, m2 * inv, m3 * inv
    pzz = at(z2, 0)
    extra = 2.0 * m0 * (ux * ux + uy * uy + uz * uz) - m4
    heat_x = 0.5 * (m10 - 2.0 * (ux * m5 + uy * m7 + uz * m8) + extra * ux)
    heat_y = 0.5 * (m11 - 2.0 * (ux * m7 + uy * m6 + uz * m9) + extra * uy)
    heat_z = 0.5 * (m12 - 2.0 * (ux * m8 + uy * m9 + uz * pzz) + extra * uz)
    return [m0, m1, m2, m3, 0.5 * m4, heat_x, heat_y, heat_z]


def advance_kernel(
    groups,
    tiles,
    dist,
    rate_ref,
    wall_ref,
    conv_out,
    rows_out,
    pad,
    conv,
    hal_send,
    hal_recv,
    part,
    gath,
    row_send,
    rows,
    tr,
    tab_x,
    tab_y,
    in_sem,
    out_sem,
    hs_sem,
    hr_sem,
    rs_send,
    rs_recv,
    ag_send,
    ag_recv,
):
    iy_count, _, _, row_count, cols = dist.shape
    vel_count = iy_count * VX
    nch = chunks_of(iy_count)
    span = iy_count // nch
    me = lax.axis_index("vel")
    here = lax.axis_index("space")
    right = lax.rem(here + 1, tiles)
    left = lax.rem(here + tiles - 1, tiles)
    iy0, iz = velocity_base(me, vel_count)
    first_owner = groups // 2 - row_count // 2
    mine = me - first_owner
    owner = jnp.logical_and(mine >= 0, mine < row_count)

    def load_in(c, sign):
        lo = row_count * sign
        return pltpu.make_async_copy(
            dist.at[pl.ds(c * span, span), sign],
            pad.at[pl.ds(c * span, span), sign, :, pl.ds(lo, row_count), :],
            in_sem.at[c, sign],
        )

    for c in range(nch):
        for sign in range(2):
            load_in(c, sign).start()

    barrier = pltpu.get_barrier_semaphore()

    def greet(p, carry):
        @pl.when(p != me)
        def _():
            pl.semaphore_signal(
                barrier, inc=1, device_id={"vel": p, "space": here}, device_id_type=MESH
            )

        for other in (left, right):
            pl.semaphore_signal(
                barrier, inc=1, device_id={"vel": p, "space": other}, device_id_type=MESH
            )
        return carry

    lax.fori_loop(0, groups, greet, 0)
    pl.semaphore_wait(barrier, 3 * groups - 1)

    def halo(it, c, sign):
        return pltpu.make_async_remote_copy(
            src_ref=hal_send.at[it, sign, pl.ds(c * span, span)],
            dst_ref=hal_recv.at[it, sign, pl.ds(c * span, span)],
            send_sem=hs_sem.at[it, sign, c],
            recv_sem=hr_sem.at[it, sign, c],
            device_id={"vel": me, "space": right if sign else left},
            device_id_type=MESH,
        )

    def send_halo(it, c):
        def pack(j, carry):
            iy = c * span + j
            for sign in range(2):
                row = 2 * row_count - 1 if sign else 0
                for k in range(0, HX, 8):
                    hal_send[it, sign, iy, pl.ds(k, 8), :] = pad[iy, sign, pl.ds(k, 8), row, :]
            return carry

        lax.fori_loop(0, span, pack, 0)
        for sign in range(2):
            halo(it, c, sign).start()

    def take_halo(it, c):
        for sign in range(2):
            halo(it, c, sign).wait_recv()

        def unpack(j, carry):
            iy = c * span + j
            for sign in range(2):
                row = row_count - 1 if sign else row_count
                for k in range(0, HX, 8):
                    pad[iy, sign, pl.ds(k, 8), row, :] = hal_recv[it, sign, iy, pl.ds(k, 8), :]
            return carry

        lax.fori_loop(0, span, unpack, 0)

    def transport(c, sums):
        def body(j, sums):
            iy = c * span + j
            iyg = iy0 + iy
            sy = speed_y(iyg)
            cy = jnp.full((row_count, cols), STEP * jnp.abs(sy), f32)
            shift = jnp.where(iyg < VY // 2, cols - 1, 1).astype(jnp.int32)

            def moved(ix):
                sign, k = ix // HX, ix % HX
                lo = row_count * sign
                cur = pad[iy, sign, k, pl.ds(lo, row_count), :]
                near = pad[iy, sign, k, pl.ds(lo - 1 if sign else lo + 1, row_count), :]
                along = pltpu.roll(cur, shift, 1)
                cx = STEP * abs(speed_x(ix))
                new = cur + cx * (near - cur) + cy * (along - cur)
                conv[iy * VX + ix] = new
                return new

            s0 = s1 = s2 = s3 = jnp.zeros((row_count, cols), f32)
            for k in range(HX):
                low, high = moved(k), moved(VX - 1 - k)
                sx = speed_x(VX - 1 - k)
                even, odd = high + low, sx * (high - low)
                s0 = s0 + even
                s1 = s1 + odd
                s2 = s2 + (sx * sx) * even
                s3 = s3 + (sx * sx) * odd
            vy = jnp.full((row_count, cols), sy, f32)
            y2 = vy * vy
            a, b, cc, d, e, f, g, h = sums
            ys0 = vy * s0
            return (
                a + s0,
                b + s1,
                cc + ys0,
                d + s2,
                e + y2 * s0,
                f + vy * s1,
                g + s3 + y2 * s1,
                h + vy * s2 + y2 * ys0,
            )

        return lax.fori_loop(0, span, body, sums)

    def copy_out(c):
        return pltpu.make_async_copy(
            conv.at[pl.ds(c * span * VX, span * VX)],
            conv_out.at[pl.ds(c * span * VX, span * VX)],
            out_sem.at[c],
        )

    def reduce_copy(it, r):
        return pltpu.make_async_remote_copy(
            src_ref=part.at[it, r],
            dst_ref=gath.at[it, me],
            send_sem=rs_send.at[it, r],
            recv_sem=rs_recv.at[it, me],
            device_id={"vel": first_owner + r, "space": here},
            device_id_type=MESH,
        )

    def row_copy(it, p, other):
        low = mine < SWEEPS
        target = jnp.where(low, left, right)
        slot = jnp.where(low, mine + SWEEPS + row_count, mine - (row_count - SWEEPS))
        if not other:
            target, slot = here, mine + SWEEPS
        return pltpu.make_async_remote_copy(
            src_ref=row_send.at[it],
            dst_ref=rows.at[it, slot],
            send_sem=ag_send.at[it, other, p],
            recv_sem=ag_recv.at[it, slot],
            device_id={"vel": p, "space": target},
            device_id_type=MESH,
        )

    def reduce(it, sums):
        for k in range(8):
            part[it, :, k, :] = sums[k] * QUAD
        for r in range(row_count):

            @pl.when(me != first_owner + r)
            def _():
                reduce_copy(it, r).start()

        @pl.when(owner)
        def _():
            gath[it, me] = part[it, mine]

            def add(i, sums):
                @pl.when(i != me)
                def _():
                    pltpu.make_async_remote_copy(
                        src_ref=part.at[it, 0],
                        dst_ref=gath.at[it, i],
                        send_sem=rs_send.at[it, 0],
                        recv_sem=rs_recv.at[it, i],
                        device_id={"vel": i, "space": here},
                        device_id_type=MESH,
                    ).wait_recv()

                sz = speed_z(velocity_base(i, vel_count)[1])
                value = gath[it, i]
                v1 = sz * value
                v2 = sz * v1
                v3 = sz * v2
                return (sums[0] + value, sums[1] + v1, sums[2] + v2, sums[3] + v3)

            zero = jnp.zeros((8, cols), f32)
            total = lax.fori_loop(0, groups, add, (zero, zero, zero, zero))
            values = heat_row(*total)
            for k in range(8):
                row_send[it, pl.ds(k, 1), :] = values[k]
            rows[it, mine + SWEEPS] = row_send[it]

            def spread(p, carry):
                @pl.when(p != me)
                def _():
                    row_copy(it, p, 0).start()

                row_copy(it, p, 1).start()
                return carry

            lax.fori_loop(0, groups, spread, 0)

    def await_rows(it):
        for slot in range(row_count + 2 * SWEEPS):

            def wait():
                pltpu.make_async_remote_copy(
                    src_ref=row_send.at[it],
                    dst_ref=rows.at[it, slot],
                    send_sem=ag_send.at[it, 0, 0],
                    recv_sem=ag_recv.at[it, slot],
                    device_id={"vel": me, "space": right},
                    device_id_type=MESH,
                ).wait_recv()

            if SWEEPS <= slot < SWEEPS + row_count:
                pl.when(me != first_owner + slot - SWEEPS)(wait)
            else:
                wait()

    zero = jnp.zeros((row_count, cols), f32)
    for it in range(ITERS):
        if it == 0:
            for c in range(nch):
                for sign in range(2):
                    load_in(c, sign).wait()
                send_halo(it, c)
        else:
            await_rows(it - 1)
            diffuse_rows(rows.at[it - 1], tr, row_count)
            keep = macro_tables(tr, rate_ref, wall_ref, tab_x, tab_y, iy0, iz, iy_count)

            def load(iy, ix):
                return conv[iy * VX + ix]

            def store(iy, ix, value):
                sign, k = ix // HX, ix % HX
                pad[iy, sign, k, pl.ds(row_count * sign, row_count), :] = value

            for c in range(nch):
                collide(load, store, tab_x, tab_y, keep, c * span, span)
                send_halo(it, c)
        sums = (zero,) * 8
        for c in range(nch):
            take_halo(it, c)
            sums = transport(c, sums)
            if it == ITERS - 1:
                copy_out(c).start()
        reduce(it, sums)
    last = ITERS - 1
    await_rows(last)
    rows_copy = pltpu.make_async_copy(rows.at[last], rows_out, out_sem.at[nch])
    rows_copy.start()
    for it in range(ITERS):
        for c in range(nch):
            for sign in range(2):
                halo(it, c, sign).wait_send()
        for r in range(row_count):

            @pl.when(me != first_owner + r)
            def _():
                reduce_copy(it, r).wait_send()

        @pl.when(owner)
        def _():
            def drain(p, carry):
                @pl.when(p != me)
                def _():
                    row_copy(it, p, 0).wait_send()

                row_copy(it, p, 1).wait_send()
                return carry

            lax.fori_loop(0, groups, drain, 0)

    for c in range(nch):
        copy_out(c).wait()
    rows_copy.wait()


def final_kernel(
    conv_in, rows, rate_ref, wall_ref, out, fields, buf, tr, tab_x, tab_y, in_sem, out_sem
):
    vel_count, row_count, cols = conv_in.shape
    iy_count = vel_count // VX
    nch = chunks_of(iy_count)
    span = iy_count // nch
    iy0, iz = velocity_base(lax.axis_index("vel"), vel_count)

    def piece(c):
        return pl.ds(c * span * VX, span * VX)

    def load_in(c):
        return pltpu.make_async_copy(conv_in.at[piece(c)], buf.at[piece(c)], in_sem.at[c])

    def copy_out(c):
        return pltpu.make_async_copy(buf.at[piece(c)], out.at[piece(c)], out_sem.at[c])

    for c in range(nch):
        load_in(c).start()
    diffuse_rows(rows, tr, row_count)
    for k in range(5):
        fields[k] = tr[:, k, :]
    keep = macro_tables(tr, rate_ref, wall_ref, tab_x, tab_y, iy0, iz, iy_count)

    def load(iy, ix):
        return buf[iy * VX + ix]

    def store(iy, ix, value):
        buf[iy * VX + ix] = value

    for c in range(nch):
        load_in(c).wait()
        collide(load, store, tab_x, tab_y, keep, c * span, span)
        copy_out(c).start()
    for c in range(nch):
        copy_out(c).wait()


def per_device(groups, tiles, distribution, rate_class, boundary_obstacle_indicator):
    vel_count, row_count, cols = distribution.shape
    iy_count = vel_count // VX
    nch = chunks_of(iy_count)
    vmem = pl.BlockSpec(memory_space=pltpu.VMEM)
    anywhere = pl.BlockSpec(memory_space=pl.ANY)
    total = row_count + 2 * SWEEPS
    tile = (row_count, cols)
    dma = pltpu.SemaphoreType.DMA
    conv, rows = pl.pallas_call(
        functools.partial(advance_kernel, groups, tiles),
        out_shape=(
            jax.ShapeDtypeStruct(distribution.shape, f32),
            jax.ShapeDtypeStruct((total, 8, cols), f32),
        ),
        in_specs=[anywhere, vmem, vmem],
        out_specs=(anywhere, anywhere),
        scratch_shapes=[
            pltpu.VMEM((iy_count, 2, HX, 2 * row_count, cols), f32),
            pltpu.VMEM((vel_count,) + tile, f32),
            pltpu.VMEM((ITERS, 2, iy_count, HX, cols), f32),
            pltpu.VMEM((ITERS, 2, iy_count, HX, cols), f32),
            pltpu.VMEM((ITERS, row_count, 8, cols), f32),
            pltpu.VMEM((ITERS, groups, 8, cols), f32),
            pltpu.VMEM((ITERS, 8, cols), f32),
            pltpu.VMEM((ITERS, total, 8, cols), f32),
            pltpu.VMEM((row_count, 8, cols), f32),
            pltpu.VMEM((3, VX) + tile, f32),
            pltpu.VMEM((3, iy_count) + tile, f32),
            dma((nch, 2)),
            dma((nch + 1,)),
            dma((ITERS, 2, nch)),
            dma((ITERS, 2, nch)),
            dma((ITERS, row_count)),
            dma((ITERS, groups)),
            dma((ITERS, 2, groups)),
            dma((ITERS, total)),
        ],
        compiler_params=pltpu.CompilerParams(collective_id=0, has_side_effects=True),
    )(
        distribution.reshape(iy_count, 2, HX, row_count, cols),
        rate_class,
        boundary_obstacle_indicator,
    )
    field, fields = pl.pallas_call(
        final_kernel,
        out_shape=(
            jax.ShapeDtypeStruct(distribution.shape, f32),
            jax.ShapeDtypeStruct((5,) + tile, f32),
        ),
        in_specs=[anywhere, vmem, vmem, vmem],
        out_specs=(anywhere, vmem),
        scratch_shapes=[
            pltpu.VMEM((vel_count,) + tile, f32),
            pltpu.VMEM((row_count, 8, cols), f32),
            pltpu.VMEM((3, VX) + tile, f32),
            pltpu.VMEM((3, iy_count) + tile, f32),
            dma((nch,)),
            dma((nch,)),
        ],
    )(conv, rows, rate_class, boundary_obstacle_indicator)
    return field, fields


def solution(mesh):
    placed = (P("vel", "space", None), P("space", None), P("space", None))
    return jax.shard_map(
        functools.partial(per_device, mesh.shape["vel"], mesh.shape["space"]),
        mesh=mesh,
        in_specs=placed,
        out_specs=(P("vel", "space", None), P(None, "space", None)),
        check_vma=False,
    )
```

time: 240 us -> 45.3 us (0.19)
  blocking collectives: 150 us -> 0 us
  Pallas kernels: 0 us -> 44.5 us
  local copies, waits for them, and re-layouts: 42.1 us -> 0 us
  other arithmetic: 35.1 us -> 0 us
  matrix products: 7.12 us -> 0 us
    psum x2 -> x0, blocking collectives: 150 us -> none  [per_device(): moments = lax.psum(partial_value, 'vel')]
    pallas_call x0 -> x2, Pallas kernels: none -> 44.5 us  [the longest x1 39.4 us: per_device(): pl.pallas_call(functools.partial(advance_kernel, groups, tiles), out_shap...]
    slice x24 -> x0, local copies, waits for them, and re-layouts: 24.5 us -> none  [the longest x4 18.6 us: transport(): from_right = jnp.roll(field, -1, 2)]
    sub x4 -> x0, other arithmetic: 17.2 us -> none  [the longest x2 17.2 us: transport(): return field - term_x - term_y]
    unnamed x18 -> x0, local copies, waits for them, and re-layouts: 16.7 us -> none
    select_n x2 -> x0, other arithmetic: 16.2 us -> none  [collision_update_piece(): return jnp.where(obstacle_indicators > 0, wall_state, relaxed)]
    dot_general x2 -> x0, matrix products: 7.12 us -> none  [per_device(): jnp.dot(weights, convected_fields.reshape(vel_count, row_count * col_coun...]
  transfers between devices with their start and end apart: 8 -> 0, of which waited for: 4 -> 0; matrix products, arithmetic and copies ran while one was open for 10% -> 0% of each run, Pallas kernels for 0% -> 0%
where the time goes in v1:
time: 45.3 us; the launch traced here: 45.1 us
  Pallas kernels  44.5 us (98%)
  between operations  0.64 us (1%)
    pallas_call x1, Pallas kernels, per_device(): pl.pallas_call(functools.partial(advance_kernel, groups, tiles), out_shap...  39.4 us
    pallas_call x1, Pallas kernels, per_device(): pl.pallas_call(final_kernel, out_shape=(jax.ShapeDtypeStruct(distribution...  5.11 us

profile of v1, /device:TPU:0, one launch (start us, length us, event | category | flops | bytes accessed | tf_op | source)
XLA Modules:
  0.0 45.1 jit_solution(11297938307543056568)
XLA Ops:
  0.6 39.4 %shard_map.50 = (f32[1024,8,128]{2,1,0:T(8,128)}, f32[16,8,128]{2,1,0:T(8,128)}) custom-call(f32[32,2,16,8,128]{4,3,2,1,0:T(8,128)} %bitcast.1, s32[8,128]{1,0:T(8,128)} %rate_ref.3, s32[8,128]{1,0:T(8,128)} %wall_ref.3), custom_call_target="tpu_custom_call" | custom-call | tf_op jit(solution)/shard_map/pallas_call | solution.py:519
  40.0 5.1 %shard_map.51 = (f32[1024,8,128]{2,1,0:T(8,128)}, f32[5,8,128]{2,1,0:T(8,128)}) custom-call(f32[1024,8,128]{2,1,0:T(8,128)} %get-tuple-element.4.conv_in, f32[16,8,128]{2,1,0:T(8,128)} %get-tuple-element.5.rows, s32[8,128]{1,0:T(8,128)} %rate_ref.3, s32[8,128]{1,0:T(8,128)} %wall_ref.3), custom_call_target="tpu_custom_call" | custom-call | tf_op jit(solution)/shard_map/pallas_call | solution.py:554

commit v2 on v1

--- a/solution.py
+++ b/solution.py
@@ -225,7 +225,21 @@
         return carry
 
     lax.fori_loop(0, groups, greet, 0)
-    pl.semaphore_wait(barrier, 3 * groups - 1)
+    flat_pad = pad.reshape(vel_count * 2 * row_count, cols)
+    flat_conv = conv.reshape(vel_count * row_count, cols)
+
+    def pad_rows(iy, sign, k, row):
+        start = ((iy * 2 + sign) * HX + k) * 2 * row_count + row
+        return pl.ds(start, 8, stride=2 * row_count)
+
+    def clear(iy, carry):
+        for sign in range(2):
+            for k in range(0, HX, 8):
+                row = row_count - 1 if sign else row_count
+                flat_pad[pad_rows(iy, sign, k, row), :] = jnp.zeros((8, cols), f32)
+        return carry
+
+    lax.fori_loop(0, iy_count, clear, 0)
 
     def halo(it, c, sign):
         return pltpu.make_async_remote_copy(
@@ -237,32 +251,67 @@
             device_id_type=MESH,
         )
 
-    def send_halo(it, c):
+    def pack_halo(it, c):
         def pack(j, carry):
             iy = c * span + j
             for sign in range(2):
                 row = 2 * row_count - 1 if sign else 0
                 for k in range(0, HX, 8):
-                    hal_send[it, sign, iy, pl.ds(k, 8), :] = pad[iy, sign, pl.ds(k, 8), row, :]
+                    hal_send[it, sign, iy, pl.ds(k, 8), :] = flat_pad[
+                        pad_rows(iy, sign, k, row), :
+                    ]
             return carry
 
         lax.fori_loop(0, span, pack, 0)
+
+    def send_halo(it, c):
         for sign in range(2):
             halo(it, c, sign).start()
 
-    def take_halo(it, c):
+    sub = lax.broadcasted_iota(jnp.int32, (8, cols), 0)
+    groups_x = [(sign, k) for sign in range(2) for k in range(0, HX, 8)]
+    group_sx = [speed_x((sub + (sign * HX + k)).astype(f32)) for sign, k in groups_x]
+
+    def fix_halo(it, c, carry):
         for sign in range(2):
             halo(it, c, sign).wait_recv()
 
-        def unpack(j, carry):
+        def body(j, carry):
             iy = c * span + j
-            for sign in range(2):
-                row = row_count - 1 if sign else row_count
-                for k in range(0, HX, 8):
-                    pad[iy, sign, pl.ds(k, 8), row, :] = hal_recv[it, sign, iy, pl.ds(k, 8), :]
-            return carry
-
-        lax.fori_loop(0, span, unpack, 0)
+            sy = jnp.full((8, cols), speed_y(iy0 + iy), f32)
+            out = []
+            for n, (sign, k) in enumerate(groups_x):
+                row = 0 if sign else row_count - 1
+                extra = STEP * jnp.abs(group_sx[n]) * hal_recv[it, sign, iy, pl.ds(k, 8), :]
+                where = pl.ds((iy * VX + sign * HX + k) * row_count + row, 8, stride=row_count)
+                flat_conv[where, :] = flat_conv[where, :] + extra
+                e1 = sy * extra
+                e2 = sy * e1
+                u = carry[n]
+                out.append((u[0] + extra, u[1] + e1, u[2] + e2, u[3] + sy * e2))
+            return tuple(out)
+
+        return lax.fori_loop(0, span, body, carry)
+
+    def add_fix(sums, carry):
+        rows_of = lax.broadcasted_iota(jnp.int32, (row_count, cols), 0)
+        for sign in range(2):
+            parts = [[] for _ in range(8)]
+            for n, (group_sign, _) in enumerate(groups_x):
+                if group_sign != sign:
+                    continue
+                x, (u0, u1, u2, u3) = group_sx[n], carry[n]
+                x0 = x * u0
+                xx0 = x * x0
+                values = (u0, x0, u1, xx0, u2, x * u1, x * (xx0 + u2), x * (x * u1) + u3)
+                for k in range(8):
+                    parts[k].append(values[k])
+            target = 0 if sign else row_count - 1
+            sums = tuple(
+                old + jnp.where(rows_of == target, jnp.sum(sum(p), axis=0, keepdims=True), 0.0)
+                for old, p in zip(sums, parts)
+            )
+        return sums
 
     def transport(c, sums):
         def body(j, sums):
@@ -409,12 +458,23 @@
                 wait()
 
     zero = jnp.zeros((row_count, cols), f32)
+    zero8 = jnp.zeros((8, cols), f32)
+    ready = nch // 2
     for it in range(ITERS):
+        sums = (zero,) * 8
         if it == 0:
             for c in range(nch):
-                for sign in range(2):
-                    load_in(c, sign).wait()
-                send_halo(it, c)
+                if c <= ready:
+                    arrived = range(c, nch) if c == ready else (c,)
+                    for d in arrived:
+                        for sign in range(2):
+                            load_in(d, sign).wait()
+                        pack_halo(it, d)
+                if c == ready:
+                    pl.semaphore_wait(barrier, 3 * groups - 1)
+                    for d in range(nch):
+                        send_halo(it, d)
+                sums = transport(c, sums)
         else:
             await_rows(it - 1)
             diffuse_rows(rows.at[it - 1], tr, row_count)
@@ -429,14 +489,15 @@
 
             for c in range(nch):
                 collide(load, store, tab_x, tab_y, keep, c * span, span)
+                pack_halo(it, c)
                 send_halo(it, c)
-        sums = (zero,) * 8
+                sums = transport(c, sums)
+        added = ((zero8,) * 4,) * len(groups_x)
         for c in range(nch):
-            take_halo(it, c)
-            sums = transport(c, sums)
+            added = fix_halo(it, c, added)
             if it == ITERS - 1:
                 copy_out(c).start()
-        reduce(it, sums)
+        reduce(it, add_fix(sums, added))
     last = ITERS - 1
     await_rows(last)
     rows_copy = pltpu.make_async_copy(rows.at[last], rows_out, out_sem.at[nch])

time: 45.3 us -> 42.2 us (0.932)
  Pallas kernels: 44.5 us -> 41.4 us
    pallas_call x1, Pallas kernels: 39.4 us -> 36.3 us  [per_device(): pl.pallas_call(functools.partial(advance_kernel, groups, tiles), out_shap...]
where the time goes in v2:
time: 42.2 us; the launch traced here: 42 us
  Pallas kernels  41.4 us (98%)
  between operations  0.64 us (2%)
    pallas_call x1, Pallas kernels, per_device(): pl.pallas_call(functools.partial(advance_kernel, groups, tiles), out_shap...  36.3 us
    pallas_call x1, Pallas kernels, per_device(): pl.pallas_call(final_kernel, out_shape=(jax.ShapeDtypeStruct(distribution...  5.11 us

profile of v2, /device:TPU:0, one launch (start us, length us, event | category | flops | bytes accessed | tf_op | source)
XLA Modules:
  0.0 42.0 jit_solution(2636811592036809851)
XLA Ops:
  0.6 36.3 %shard_map.50 = (f32[1024,8,128]{2,1,0:T(8,128)}, f32[16,8,128]{2,1,0:T(8,128)}) custom-call(f32[32,2,16,8,128]{4,3,2,1,0:T(8,128)} %bitcast.1, s32[8,128]{1,0:T(8,128)} %rate_ref.3, s32[8,128]{1,0:T(8,128)} %wall_ref.3), custom_call_target="tpu_custom_call" | custom-call | tf_op jit(solution)/shard_map/pallas_call | solution.py:580
  36.9 5.1 %shard_map.51 = (f32[1024,8,128]{2,1,0:T(8,128)}, f32[5,8,128]{2,1,0:T(8,128)}) custom-call(f32[1024,8,128]{2,1,0:T(8,128)} %get-tuple-element.4.conv_in, f32[16,8,128]{2,1,0:T(8,128)} %get-tuple-element.5.rows, s32[8,128]{1,0:T(8,128)} %rate_ref.3, s32[8,128]{1,0:T(8,128)} %wall_ref.3), custom_call_target="tpu_custom_call" | custom-call | tf_op jit(solution)/shard_map/pallas_call | solution.py:615

commit v3 on v2

--- a/solution.py
+++ b/solution.py
@@ -95,7 +95,7 @@
         tab_x[2, ix] = jnp.where(wall, zero, x2)
         return carry
 
-    lax.fori_loop(0, VX, table_x, 0, unroll=4)
+    lax.fori_loop(0, VX, table_x, 0, unroll=16)
 
     def table_y(iy, carry):
         sy = jnp.full(density.shape, speed_y(iy0 + iy), f32)
@@ -108,7 +108,7 @@
         tab_y[2, iy] = jnp.where(wall, zero, y2 + z2 - 5.0)
         return carry
 
-    lax.fori_loop(0, iy_count, table_y, 0, unroll=min(4, iy_count))
+    lax.fori_loop(0, iy_count, table_y, 0, unroll=min(16, iy_count))
     return jnp.where(wall, zero, 1.0 - rate)
 
 
@@ -262,7 +262,7 @@
                     ]
             return carry
 
-        lax.fori_loop(0, span, pack, 0)
+        lax.fori_loop(0, span, pack, 0, unroll=min(4, span))
 
     def send_halo(it, c):
         for sign in range(2):
@@ -291,7 +291,7 @@
                 out.append((u[0] + extra, u[1] + e1, u[2] + e2, u[3] + sy * e2))
             return tuple(out)
 
-        return lax.fori_loop(0, span, body, carry)
+        return lax.fori_loop(0, span, body, carry, unroll=2)
 
     def add_fix(sums, carry):
         rows_of = lax.broadcasted_iota(jnp.int32, (row_count, cols), 0)
@@ -314,12 +314,13 @@
         return sums
 
     def transport(c, sums):
-        def body(j, sums):
+        def body(shift, j, sums):
             iy = c * span + j
             iyg = iy0 + iy
             sy = speed_y(iyg)
             cy = jnp.full((row_count, cols), STEP * jnp.abs(sy), f32)
-            shift = jnp.where(iyg < VY // 2, cols - 1, 1).astype(jnp.int32)
+
+            rest = 1.0 - cy
 
             def moved(ix):
                 sign, k = ix // HX, ix % HX
@@ -328,7 +329,7 @@
                 near = pad[iy, sign, k, pl.ds(lo - 1 if sign else lo + 1, row_count), :]
                 along = pltpu.roll(cur, shift, 1)
                 cx = STEP * abs(speed_x(ix))
-                new = cur + cx * (near - cur) + cy * (along - cur)
+                new = cur * (rest - cx) + cx * near + cy * along
                 conv[iy * VX + ix] = new
                 return new
 
@@ -356,7 +357,14 @@
                 h + vy * s2 + y2 * ys0,
             )
 
-        return lax.fori_loop(0, span, body, sums)
+        half = span // 2
+        below = jnp.clip(lax.div(VY // 2 - iy0 - c * span, 2), 0, half)
+
+        def pair(shift, j, sums):
+            return body(shift, 2 * j + 1, body(shift, 2 * j, sums))
+
+        sums = lax.fori_loop(0, below, functools.partial(pair, cols - 1), sums)
+        return lax.fori_loop(below, half, functools.partial(pair, 1), sums)
 
     def copy_out(c):
         return pltpu.make_async_copy(
@@ -423,7 +431,7 @@
                 return (sums[0] + value, sums[1] + v1, sums[2] + v2, sums[3] + v3)
 
             zero = jnp.zeros((8, cols), f32)
-            total = lax.fori_loop(0, groups, add, (zero, zero, zero, zero))
+            total = lax.fori_loop(0, groups, add, (zero, zero, zero, zero), unroll=min(16, groups))
             values = heat_row(*total)
             for k in range(8):
                 row_send[it, pl.ds(k, 1), :] = values[k]
@@ -437,7 +445,7 @@
                 row_copy(it, p, 1).start()
                 return carry
 
-            lax.fori_loop(0, groups, spread, 0)
+            lax.fori_loop(0, groups, spread, 0, unroll=4)
 
     def await_rows(it):
         for slot in range(row_count + 2 * SWEEPS):
@@ -459,7 +467,7 @@
 
     zero = jnp.zeros((row_count, cols), f32)
     zero8 = jnp.zeros((8, cols), f32)
-    ready = nch // 2
+    ready = nch - 1
     for it in range(ITERS):
         sums = (zero,) * 8
         if it == 0:

time: 42.2 us -> 39.7 us (0.941)
  Pallas kernels: 41.4 us -> 38.8 us
    pallas_call x1, Pallas kernels: 36.3 us -> 33.7 us  [per_device(): pl.pallas_call(functools.partial(advance_kernel, groups, tiles), out_shap...]
where the time goes in v3:
time: 39.7 us; the launch traced here: 39.4 us
  Pallas kernels  38.8 us (98%)
  between operations  0.64 us (2%)
    pallas_call x1, Pallas kernels, per_device(): pl.pallas_call(functools.partial(advance_kernel, groups, tiles), out_shap...  33.7 us
    pallas_call x1, Pallas kernels, per_device(): pl.pallas_call(final_kernel, out_shape=(jax.ShapeDtypeStruct(distribution...  5.06 us

profile of v3, /device:TPU:0, one launch (start us, length us, event | category | flops | bytes accessed | tf_op | source)
XLA Modules:
  0.0 39.4 jit_solution(16399260589854272761)
XLA Ops:
  0.6 33.7 %shard_map.50 = (f32[1024,8,128]{2,1,0:T(8,128)}, f32[16,8,128]{2,1,0:T(8,128)}) custom-call(f32[32,2,16,8,128]{4,3,2,1,0:T(8,128)} %bitcast.1, s32[8,128]{1,0:T(8,128)} %rate_ref.3, s32[8,128]{1,0:T(8,128)} %wall_ref.3), custom_call_target="tpu_custom_call" | custom-call | tf_op jit(solution)/shard_map/pallas_call | solution.py:588
  34.4 5.1 %shard_map.51 = (f32[1024,8,128]{2,1,0:T(8,128)}, f32[5,8,128]{2,1,0:T(8,128)}) custom-call(f32[1024,8,128]{2,1,0:T(8,128)} %get-tuple-element.4.conv_in, f32[16,8,128]{2,1,0:T(8,128)} %get-tuple-element.5.rows, s32[8,128]{1,0:T(8,128)} %rate_ref.3, s32[8,128]{1,0:T(8,128)} %wall_ref.3), custom_call_target="tpu_custom_call" | custom-call | tf_op jit(solution)/shard_map/pallas_call | solution.py:623
